TPU v7x, 32 devices: a whole 2x2x4 slice. The times are simulated.
32 devices in a mesh: fsdp: 8 (over z, y), rep: 4 (over x, core).
Axes of the slice: x: 2, y: 2, z: 4, core: 2. Of those that a mesh axis runs over, the one named last changes fastest.
Arguments:
- layer_input: bfloat16 [64, 512, 768], P(('fsdp', 'rep')), may hold values from -6 to 6
- segment_ids: int32 [64, 512], P(('fsdp', 'rep')), may hold values from 0 to 511, as said below
- joint_weight: bfloat16 [768, 2304], P('fsdp'), may hold values from -0.21875 to 0.21875
- query_bias: bfloat16 [768], replicated, may hold values from -3 to 3
- value_bias: bfloat16 [768], replicated, may hold values from -3 to 3
- close_weight: bfloat16 [768, 768], P('fsdp'), may hold values from -0.875 to 0.875
- close_bias: bfloat16 [768], replicated, may hold values from -3 to 3
- first_gain: bfloat16 [768], replicated, may hold values from 0.099609375 to 1.8984375
- first_shift: bfloat16 [768], replicated, may hold values from -3 to 3
- expand_weight: bfloat16 [768, 3072], P('fsdp'), may hold values from -0.21875 to 0.21875
- expand_bias: bfloat16 [3072], replicated, may hold values from -3 to 3
- shrink_weight: bfloat16 [3072, 768], P('fsdp'), may hold values from -0.109375 to 0.109375
- shrink_bias: bfloat16 [768], replicated, may hold values from -3 to 3
- second_gain: bfloat16 [768], replicated, may hold values from 0.099609375 to 1.8984375
- second_shift: bfloat16 [768], replicated, may hold values from -3 to 3
- cotangent: bfloat16 [64, 512, 768], P(('fsdp', 'rep')), may hold values from -6 to 6
Outputs:
- layer_output: bfloat16 [64, 512, 768], P(('fsdp', 'rep'))
- input_grad: float32 [64, 512, 768], P(('fsdp', 'rep'))
- joint_grad: float32 [768, 2304], P('fsdp')
- query_bias_grad: float32 [768], replicated
- value_bias_grad: float32 [768], replicated
- close_grad: float32 [768, 768], P('fsdp')
- close_bias_grad: float32 [768], replicated
- first_gain_grad: float32 [768], replicated
- first_shift_grad: float32 [768], replicated
- expand_grad: float32 [768, 3072], P('fsdp')
- expand_bias_grad: float32 [3072], replicated
- shrink_grad: float32 [3072, 768], P('fsdp')
- shrink_bias_grad: float32 [768], replicated
- second_gain_grad: float32 [768], replicated
- second_shift_grad: float32 [768], replicated
Inputs may be any that keep to these rules, and one draw needn't show every extreme that they name: `segment_ids`: along each packed row of 512 positions the document numbers start at 0, never fall and rise by at most one from a position to the next; every position belongs to a document. Some row holds 512 documents of one position.
All inputs are finite; a program needn't handle non-finite values.
Results may differ from a plain program's by a relative error of at most 0.015.
Values may be sent and summed in bfloat16 or wider, within the bound.
No kernel may reach another device: no remote copies, remote signals or barrier semaphores. Data moves between devices by JAX's collectives and lax.ppermute only.
A program may use at most 192 MiB of HBM per device.

v0:
```python
import math
import jax
import jax.numpy as jnp
from jax import lax
from jax.sharding import PartitionSpec as P

HEADS = 12
EPS = 1e-12


def layer_norm(values, gain, shift):
    average = jnp.mean(values, axis=-1, keepdims=True)
    centred = values - average
    variance = jnp.mean(centred * centred, axis=-1, keepdims=True)
    return centred * lax.rsqrt(variance + EPS) * gain + shift


def gelu_exact(values):
    return jax.nn.gelu(values, approximate=False)


def split_heads(packed):
    pos_count = packed.shape[0]
    model_width = packed.shape[1] // 3
    head_size = model_width // HEADS
    queries = packed[:, :model_width].reshape(pos_count, HEADS, head_size)
    keys_part = packed[:, model_width : 2 * model_width].reshape(pos_count, HEADS, head_size)
    values_part = packed[:, 2 * model_width :].reshape(pos_count, HEADS, head_size)
    return (queries, keys_part, values_part, 1.0 / math.sqrt(head_size))


def masked_scores(queries, keys_part, segments, score_scale):
    scores = (
        jnp.einsum("qhd,khd->hqk", queries, keys_part, preferred_element_type=jnp.float32)
        * score_scale
    )
    same_doc = segments[:, None] == segments[None, :]
    return jnp.where(same_doc[None], scores, -jnp.inf)


def attend_row(packed, segments):
    queries, keys_part, values_part, score_scale = split_heads(packed)
    scores = masked_scores(queries, keys_part, segments, score_scale)
    top_score = jnp.max(scores, axis=-1, keepdims=True)
    raised = jnp.exp(scores - top_score)
    denominator = jnp.sum(raised, axis=-1, keepdims=True)
    attn_low = (raised / denominator).astype(jnp.bfloat16)
    context = jnp.einsum("hqk,khd->qhd", attn_low, values_part, preferred_element_type=jnp.float32)
    return (
        context.reshape(packed.shape[0], packed.shape[1] // 3),
        top_score + jnp.log(denominator),
    )


def attend_back(packed, segments, log_total, grad_context):
    pos_count = packed.shape[0]
    model_width = packed.shape[1] // 3
    queries, keys_part, values_part, score_scale = split_heads(packed)
    scores = masked_scores(queries, keys_part, segments, score_scale)
    attn_weights = jnp.exp(scores - log_total)
    grad_heads = grad_context.reshape(pos_count, HEADS, model_width // HEADS)
    grad_attn = jnp.einsum(
        "qhd,khd->hqk", grad_heads, values_part, preferred_element_type=jnp.float32
    )
    inner_sum = jnp.sum(grad_attn * attn_weights, axis=-1, keepdims=True)
    grad_scores = (attn_weights * (grad_attn - inner_sum)).astype(jnp.bfloat16)
    grad_queries = (
        jnp.einsum("hqk,khd->qhd", grad_scores, keys_part, preferred_element_type=jnp.float32)
        * score_scale
    )
    grad_keys = (
        jnp.einsum("hqk,qhd->khd", grad_scores, queries, preferred_element_type=jnp.float32)
        * score_scale
    )
    grad_values = jnp.einsum(
        "hqk,qhd->khd",
        attn_weights.astype(jnp.bfloat16),
        grad_heads,
        preferred_element_type=jnp.float32,
    )
    return jnp.concatenate(
        [
            grad_queries.reshape(pos_count, model_width),
            grad_keys.reshape(pos_count, model_width),
            grad_values.reshape(pos_count, model_width),
        ],
        axis=1,
    )


def body(
    layer_input,
    segment_ids,
    joint_weight,
    query_bias,
    value_bias,
    close_weight,
    close_bias,
    first_gain,
    first_shift,
    expand_weight,
    expand_bias,
    shrink_weight,
    shrink_bias,
    second_gain,
    second_shift,
    cotangent,
):
    row_count, pos_count, model_width = layer_input.shape
    tok_count = row_count * pos_count
    flat_input = layer_input.reshape(tok_count, model_width)
    joint_full, close_full = (
        lax.all_gather(joint_weight, "fsdp", axis=0, tiled=True),
        lax.all_gather(close_weight, "fsdp", axis=0, tiled=True),
    )
    joint_bias = jnp.concatenate([query_bias, jnp.zeros_like(query_bias), value_bias]).astype(
        jnp.float32
    )
    mixed = jnp.dot(flat_input, joint_full, preferred_element_type=jnp.float32) + joint_bias
    joint_low = mixed.astype(jnp.bfloat16).reshape(row_count, pos_count, 3 * model_width)
    context, log_total = lax.map(
        lambda packet: attend_row(packet[0], packet[1]), (joint_low, segment_ids)
    )
    context_low = context.reshape(tok_count, model_width).astype(jnp.bfloat16)
    expand_full, shrink_full = (
        lax.all_gather(expand_weight, "fsdp", axis=0, tiled=True),
        lax.all_gather(shrink_weight, "fsdp", axis=0, tiled=True),
    )
    branch = jnp.dot(
        context_low, close_full, preferred_element_type=jnp.float32
    ) + close_bias.astype(jnp.float32)
    first_sum = flat_input.astype(jnp.float32) + branch
    hidden, first_pull = jax.vjp(
        layer_norm, first_sum, first_gain.astype(jnp.float32), first_shift.astype(jnp.float32)
    )
    hidden_low = hidden.astype(jnp.bfloat16)
    inner = jnp.dot(
        hidden_low, expand_full, preferred_element_type=jnp.float32
    ) + expand_bias.astype(jnp.float32)
    active, gelu_pull = jax.vjp(gelu_exact, inner)
    active_low = active.astype(jnp.bfloat16)
    ffn_out = jnp.dot(
        active_low, shrink_full, preferred_element_type=jnp.float32
    ) + shrink_bias.astype(jnp.float32)
    output, second_pull = jax.vjp(
        layer_norm,
        hidden + ffn_out,
        second_gain.astype(jnp.float32),
        second_shift.astype(jnp.float32),
    )
    layer_output = output.astype(jnp.bfloat16).reshape(row_count, pos_count, model_width)
    expand_back, shrink_back = (
        lax.all_gather(expand_weight, "fsdp", axis=0, tiled=True),
        lax.all_gather(shrink_weight, "fsdp", axis=0, tiled=True),
    )
    grad_second, second_gain_part, second_shift_part = second_pull(
        cotangent.reshape(tok_count, model_width).astype(jnp.float32)
    )
    grad_ffn = grad_second.astype(jnp.bfloat16)
    shrink_term = jnp.einsum("tf,td->fd", active_low, grad_ffn, preferred_element_type=jnp.float32)
    grad_active = jnp.einsum("td,fd->tf", grad_ffn, shrink_back, preferred_element_type=jnp.float32)
    grad_inner = gelu_pull(grad_active)[0].astype(jnp.bfloat16)
    expand_term = jnp.einsum(
        "td,tf->df", hidden_low, grad_inner, preferred_element_type=jnp.float32
    )
    grad_hidden = grad_second + jnp.einsum(
        "tf,df->td", grad_inner, expand_back, preferred_element_type=jnp.float32
    )
    expand_part, shrink_part = (
        lax.psum_scatter(expand_term, "fsdp", scatter_dimension=0, tiled=True),
        lax.psum_scatter(shrink_term, "fsdp", scatter_dimension=0, tiled=True),
    )
    grad_first, first_gain_part, first_shift_part = first_pull(grad_hidden)
    grad_branch = grad_first.astype(jnp.bfloat16)
    joint_back, close_back = (
        lax.all_gather(joint_weight, "fsdp", axis=0, tiled=True),
        lax.all_gather(close_weight, "fsdp", axis=0, tiled=True),
    )
    close_term = jnp.einsum(
        "td,te->de", context_low, grad_branch, preferred_element_type=jnp.float32
    )
    grad_context = jnp.einsum(
        "te,de->td", grad_branch, close_back, preferred_element_type=jnp.float32
    ).astype(jnp.bfloat16)
    grad_mixed = lax.map(
        lambda packet: attend_back(packet[0], packet[1], packet[2], packet[3]),
        (
            joint_low,
            segment_ids,
            log_total,
            grad_context.reshape(row_count, pos_count, model_width),
        ),
    )
    grad_mixed_low = grad_mixed.reshape(tok_count, 3 * model_width).astype(jnp.bfloat16)
    joint_term = jnp.einsum(
        "td,te->de", flat_input, grad_mixed_low, preferred_element_type=jnp.float32
    )
    input_grad = grad_first + jnp.einsum(
        "te,de->td", grad_mixed_low, joint_back, preferred_element_type=jnp.float32
    )
    joint_part, close_part = (
        lax.psum_scatter(joint_term, "fsdp", scatter_dimension=0, tiled=True),
        lax.psum_scatter(close_term, "fsdp", scatter_dimension=0, tiled=True),
    )
    joint_grad, close_grad, expand_grad, shrink_grad = (
        lax.psum(joint_part.astype(jnp.bfloat16), "rep").astype(jnp.float32),
        lax.psum(close_part.astype(jnp.bfloat16), "rep").astype(jnp.float32),
        lax.psum(expand_part.astype(jnp.bfloat16), "rep").astype(jnp.float32),
        lax.psum(shrink_part.astype(jnp.bfloat16), "rep").astype(jnp.float32),
    )
    grad_mixed_wide = grad_mixed_low.astype(jnp.float32)
    vector_terms = (
        jnp.sum(grad_mixed_wide[:, :model_width], axis=0),
        jnp.sum(grad_mixed_wide[:, 2 * model_width :], axis=0),
        jnp.sum(grad_branch.astype(jnp.float32), axis=0),
        first_gain_part,
        first_shift_part,
        jnp.sum(grad_inner.astype(jnp.float32), axis=0),
        jnp.sum(grad_ffn.astype(jnp.float32), axis=0),
        second_gain_part,
        second_shift_part,
    )
    (
        query_bias_grad,
        value_bias_grad,
        close_bias_grad,
        first_gain_grad,
        first_shift_grad,
        expand_bias_grad,
        shrink_bias_grad,
        second_gain_grad,
        second_shift_grad,
    ) = lax.psum(
        (
            vector_terms[0],
            vector_terms[1],
            vector_terms[2],
            vector_terms[3],
            vector_terms[4],
            vector_terms[5],
            vector_terms[6],
            vector_terms[7],
            vector_terms[8],
        ),
        ("fsdp", "rep"),
    )
    return (
        layer_output,
        input_grad.reshape(row_count, pos_count, model_width),
        joint_grad,
        query_bias_grad,
        value_bias_grad,
        close_grad,
        close_bias_grad,
        first_gain_grad,
        first_shift_grad,
        expand_grad,
        expand_bias_grad,
        shrink_grad,
        shrink_bias_grad,
        second_gain_grad,
        second_shift_grad,
    )


def solution(mesh):
    placed = (
        P(("fsdp", "rep"), None, None),
        P(("fsdp", "rep"), None),
        P("fsdp", None),
        P(),
        P(),
        P("fsdp", None),
        P(),
        P(),
        P(),
        P("fsdp", None),
        P(),
        P("fsdp", None),
        P(),
        P(),
        P(),
        P(("fsdp", "rep"), None, None),
    )
    return jax.shard_map(
        body,
        mesh=mesh,
        in_specs=placed,
        out_specs=(
            P(("fsdp", "rep"), None, None),
            P(("fsdp", "rep"), None, None),
            P("fsdp", None),
            P(),
            P(),
            P("fsdp", None),
            P(),
            P(),
            P(),
            P("fsdp", None),
            P(),
            P("fsdp", None),
            P(),
            P(),
            P(),
        ),
        check_vma=False,
    )
```

profile of v0, /device:TPU:0, one launch (start us, length us, event | category | flops | bytes accessed | tf_op | source)
XLA Modules:
  0.0 939.9 jit_solution(8562727655183991149)
XLA Ops:
  19.7 57.8 %all-gather.5.cloned.1.call-done = bf16[768,2304]{1,0:T(8,128)(2,1)} async-done(((bf16[96,2304]{1,0:T(8,128)(2,1)}), bf16[768,2304]{1,0:T(8,128)(2,1)}) %all-gather.5.cloned.1.call-update) | async-done | bytes 3538960 | tf_op jit(solution)/shard_map/all_gather | solution.py:113
  77.5 8.4 add_convert_fusion.1
  86.0 6.8 copy.54
  92.8 23.4 %while.22 = (s32[]{:T(128)}, bf16[2,512,768]{2,1,0:T(8,128)(2,1)}, f32[2,12,512,1]{2,1,3,0:T(8,128)S(1)}, bf16[2,512,2304]{1,2,0:T(8,128)(2,1)}, s32[2,512]{1,0:T(2,128)S(1)}, /*index=5*/s32[]{:T(128)}) while((s32[]{:T(128)}, bf16[2,512,768]{2,1,0:T(8,128)(2,1)}, f32[2,12,512,1]{2,1,3,0:T(8,128)S(1)}, bf16[2,512,2304]{1,2,0:T(8,128)(2,1)}, ...), condition=%wide.region_3.4_spmd, body=%wide.region_0.3_spmd.sunk | while | flops 843311104 | bytes 54753372 | solution.py:121
  99.6 3.6 fusion.98
  111.3 3.6 fusion.98
  116.2 3.4 all-gather.7.cloned.1.call-done
  119.6 3.8 fusion.33
  124.0 75.9 %all-gather.9.cloned.1.call-done = bf16[768,3072]{1,0:T(8,128)(2,1)} async-done(((bf16[96,3072]{1,0:T(8,128)(2,1)}), bf16[768,3072]{1,0:T(8,128)(2,1)}) %all-gather.9.cloned.1.call-update) | async-done | bytes 4718608 | tf_op jit(solution)/shard_map/all_gather | solution.py:126
  199.8 36.0 %multiply_convert_fusion.1 = (bf16[1024,3072]{1,0:T(8,128)(2,1)}, f32[1024,3072]{1,0:T(8,128)}, f32[1024,3072]{1,0:T(8,128)}) fusion(f32[3072]{0:T(1024)S(1)} %copy-done.28, bf16[768,3072]{1,0:T(8,128)(2,1)} %all-gather.9.cloned.1.call-done, f32[1024,768]{1,0:T(8,128)S(1)} %get-tuple-element.220, f32[768]{0:T(1024)S(1)} %copy-done.19, ...), kind=kOutput, calls=%fused_computation.34 | convolution fusion | flops 5043388416 | bytes 39348224 | tf_op jit(solution)/shard_map/dot_general | solution.py:137
  235.8 43.8 %all-gather.11.cloned.1.call-done = bf16[3072,768]{1,0:T(8,128)(2,1)} async-done(((bf16[384,768]{1,0:T(8,128)(2,1)}), bf16[3072,768]{1,0:T(8,128)(2,1)}) %all-gather.11.cloned.1.call-update) | async-done | bytes 4718608 | tf_op jit(solution)/shard_map/all_gather | solution.py:127
  279.6 8.9 fusion.34
  295.5 19.4 %convert_reduce_fusion = (f32[3072]{0:T(1024)}, bf16[1024,3072]{1,0:T(8,128)(2,1)}) fusion(f32[1024,3072]{1,0:T(8,128)} %get-tuple-element.207, bf16[1024,768]{1,0:T(8,128)(2,1)} %get-tuple-element.199, bf16[3072,768]{1,0:T(8,128)(2,1)} %all-gather.11.cloned.1.call-done, f32[1024,3072]{1,0:T(8,128)} %get-tuple-element.221, f32[3072]{0:T(1024)S(1)} %copy-done.28), kind=kOutput, calls=%fused_computation.32 | convolution fusion | flops 4885312512 | bytes 37773312 | tf_op jit(solution)/shard_map/td,fd->tf/dot_general | solution.py:161
  315.0 10.1 %multiply_reduce_fusion.1 = (f32[768]{0:T(1024)}, f32[1024]{0:T(1024)S(1)}, f32[768]{0:T(1024)}, f32[1024,768]{1,0:T(8,128)S(1)}) fusion(f32[1024,768]{1,0:T(8,128)S(1)} %get-tuple-element.220, f32[1024]{0:T(1024)S(1)} %fusion.22, f32[1024]{0:T(1024)S(1)} %broadcast_multiply_fusion.1, f32[768]{0:T(1024)S(1)} %copy-done.15, ...), kind=kOutput, calls=%fused_computation.62 | convolution fusion | flops 4839699456 | bytes 20472832 | tf_op jit(solution)/shard_map/tf,df->td/dot_general | solution.py:166
  334.9 62.1 %while.23 = (s32[]{:T(128)}, bf16[2,512,2304]{2,1,0:T(8,128)(2,1)}, bf16[2,512,2304]{1,2,0:T(8,128)(2,1)}, s32[2,512]{1,0:T(2,128)S(1)}, f32[2,12,512,1]{2,1,3,0...) while((s32[]{:T(128)}, bf16[2,512,2304]{2,1,0:T(8,128)(2,1)}, ...), condition=%wide.region_14.15_spmd, body=%wide.region_12.14_spmd.sunk | while | flops 2069358592 | bytes 142784688 | solution.py:185
  339.5 3.2 fusion.111
  342.7 6.9 multiply_reduce_fusion.6
  349.5 7.1 multiply_convert_fusion.3
  362.5 3.3 constant_dynamic-update-slice_fusion.5
  373.4 6.9 multiply_reduce_fusion.6
  380.3 7.2 multiply_convert_fusion.3
  393.4 3.4 constant_dynamic-update-slice_fusion.5
  397.0 9.7 %convolution_bitcast_fusion = f32[768,2304]{0,1:T(8,128)} fusion(bf16[2,512,2304]{2,1,0:T(8,128)(2,1)} %get-tuple-element.77, bf16[2,512,768]{2,1,0:T(8,128)(2,1)} %param.20), kind=kOutput, calls=%fused_computation.49 | convolution fusion | flops 3623878656 | bytes 13369344 | tf_op jit(solution)/shard_map/td,te->de/dot_general | solution.py:195
  406.7 8.1 copy.66
  416.6 10.7 %fusion.24 = f32[768,3072]{1,0:T(8,128)} fusion(bf16[1024,3072]{1,0:T(8,128)(2,1)} %get-tuple-element.226, f32[1024,768]{1,0:T(8,128)S(1)} %copy-done.1, f32[768]{0:T(1024)S(1)} %copy-done.20, f32[768]{0:T(1024)S(1)} %copy-done.16, f32[1024]{0:T(1024)S(1)} %copy-done.14, f32[1024]{0:T(1024)S(1)} %copy-done.12), kind=kOutput, calls=%fused_computation.89 | convolution fusion | flops 4835770368 | bytes 18888704 | tf_op jit(solution)/shard_map/td,tf->df/dot_general | solution.py:163
  428.7 10.2 %fusion.37 = f32[3072,768]{1,0:T(8,128)} fusion(bf16[1024,3072]{1,0:T(8,128)(2,1)} %get-tuple-element.206, bf16[1024,768]{1,0:T(8,128)(2,1)S(1)} %copy-done.8), kind=kOutput, calls=%fused_computation.99 | convolution fusion | flops 4831838208 | bytes 17301504 | tf_op jit(solution)/shard_map/tf,td->fd/dot_general | solution.py:160
  444.5 43.5 %all-reduce = (f32[768]{0:T(1024)}, f32[768]{0:T(1024)}, f32[768]{0:T(1024)}, f32[768]{0:T(1024)}, f32[768]{0:T(1024)}, /*index=5*/f32[3072]{0:T(1024)}, f32[768]{0:T(1024)}, f32[768]{0:T(1024)}, f32[768]{0:T(1024)}) all-reduce(f32[768]{0:T(1024)S(1)} %get-tuple-element.157, ...), channel_id=1, replica_groups=mesh['fsdp'=8,'rep'=4] {'fsdp','rep'}, use_global_device_ids=true, to_apply=%region_18.19 | all-reduce | flops 9216 | bytes 73728 | tf_op jit(solution)/shard_map/psum | solution.py:233
  489.6 54.0 %reduce-scatter.13.cloned.1.call-done = f32[96,2304]{1,0:T(8,128)} async-done(((f32[768,2304]{1,0:T(8,128)}), f32[96,2304]{1,0:T(8,128)}) %reduce-scatter.13.cloned.1.call-update) | async-done | bytes 884752
  545.9 162.6 %reduce-scatter.9.cloned.1.call-done = f32[96,3072]{1,0:T(8,128)} async-done(((f32[768,3072]{1,0:T(8,128)}), f32[96,3072]{1,0:T(8,128)}) %reduce-scatter.9.cloned.1.call-update) | async-done | bytes 1179664 | tf_op jit(solution)/shard_map/reduce_scatter | solution.py:170
  710.6 162.7 %reduce-scatter.11.cloned.1.call-done = f32[384,768]{1,0:T(8,128)} async-done(((f32[3072,768]{1,0:T(8,128)}), f32[384,768]{1,0:T(8,128)}) %reduce-scatter.11.cloned.1.call-update) | async-done | bytes 1179664 | tf_op jit(solution)/shard_map/reduce_scatter | solution.py:171
  875.5 8.9 add_add_fusion.4
  884.5 40.4 %all-reduce.4.cloned.1.call-done = (bf16[96,2304]{0,1:T(8,128)(2,1)}, bf16[96,768]{1,0:T(8,128)(2,1)}, bf16[96,3072]{1,0:T(8,128)(2,1)}, bf16[384,768]{1,0:T(8,128)(2,1)}) async-done(((bf16[96,2304]{0,1:T(8,128)(2,1)}, bf16[96,768]{1,0:T(8,128)(2,1)}, bf16[96,3072]{1,0:T(8,128)(2,1)}, bf16[384,768]{1,0:T(8,128)(2,1)}), (bf16[96,2304]{0,1:T(8,128)(2,1)}, bf16[96,768]{1,0:T(8,128)(2,1)}, ...) | async-done | bytes 1769488 | tf_op jit(solution)/shard_map/psum | solution.py:206
  (176 shorter events, 94.5 us)
Async XLA Ops:
  7.2 70.3 %all-gather.5.cloned.1.call-start = ((), (), s32[]{:S(2)}) async-start(), calls=%async_computation.4 | async-start | bytes 3981312 | tf_op jit(solution)/shard_map/all_gather | solution.py:113
  7.9 111.7 %all-gather.7.cloned.1.call-start = ((), (), s32[]{:S(2)}) async-start(), calls=%async_computation.5 | async-start | bytes 1327104 | tf_op jit(solution)/shard_map/all_gather | solution.py:114
  8.7 191.2 %all-gather.9.cloned.1.call-start = ((), (), s32[]{:S(2)}) async-start(), calls=%async_computation.6 | async-start | bytes 5308416 | tf_op jit(solution)/shard_map/all_gather | solution.py:126
  9.4 270.2 %all-gather.11.cloned.1.call-start = ((), (), s32[]{:S(2)}) async-start(), calls=%async_computation.7 | async-start | bytes 5308416 | tf_op jit(solution)/shard_map/all_gather | solution.py:127
  10.0 478.0 %reduce-scatter.7.cloned.1.call-start = ((), (), s32[]{:S(2)}) async-start(), calls=%async_computation.8 | async-start | bytes 2654208 | tf_op jit(solution)/shard_map/reduce_scatter | solution.py:203
  86.0 6.8 copy-start.17
  92.8 26.8 %copy-start.31 = (f32[768]{0:T(1024)S(1)}, f32[768]{0:T(1024)}, u32[]{:S(2)}) copy-start(f32[768]{0:T(1024)} %convert_element_type.127) | copy-start | bytes 9220
  116.2 3.4 copy-start.9
  119.6 80.2 %copy-start.15 = (f32[768]{0:T(1024)S(1)}, f32[768]{0:T(1024)}, u32[]{:S(2)}) copy-start(f32[768]{0:T(1024)} %convert_element_type.128) | copy-start | bytes 9220
  119.6 80.2 %copy-start.19 = (f32[768]{0:T(1024)S(1)}, f32[768]{0:T(1024)}, u32[]{:S(2)}) copy-start(f32[768]{0:T(1024)} %convert_element_type.129) | copy-start | bytes 9220
  119.6 80.2 %copy-start.28 = (f32[3072]{0:T(1024)S(1)}, f32[3072]{0:T(1024)}, u32[]{:S(2)}) copy-start(f32[3072]{0:T(1024)} %convert_element_type.131) | copy-start | bytes 36868
  123.4 201.7 %copy-start = (f32[1024,768]{1,0:T(8,128)}, f32[1024,768]{1,0:T(8,128)S(1)}, u32[]{:S(2)}) copy-start(f32[1024,768]{1,0:T(8,128)S(1)} %get-tuple-element.220) | copy-start | bytes 9437188
  123.4 201.7 %copy-start.11 = (f32[1024]{0:T(1024)}, f32[1024]{0:T(1024)S(1)}, u32[]{:S(2)}) copy-start(f32[1024]{0:T(1024)S(1)} %broadcast_multiply_fusion.1) | copy-start | bytes 12292
  123.9 201.2 %copy-start.13 = (f32[1024]{0:T(1024)}, f32[1024]{0:T(1024)S(1)}, u32[]{:S(2)}) copy-start(f32[1024]{0:T(1024)S(1)} %fusion.22) | copy-start | bytes 12292
  123.9 155.6 %copy-start.30 = (f32[768]{0:T(1024)S(1)}, f32[768]{0:T(1024)}, u32[]{:S(2)}) copy-start(f32[768]{0:T(1024)} %convert_element_type.133) | copy-start | bytes 9220
  279.6 9.5 %copy-start.2 = (bf16[2,512,768]{2,1,0:T(8,128)(2,1)S(1)}, bf16[2,512,768]{2,1,0:T(8,128)(2,1)}, u32[]{:S(2)}) copy-start(bf16[2,512,768]{2,1,0:T(8,128)(2,1)} %param.35) | copy-start | bytes 4718596
  279.6 9.5 %copy-start.21 = (f32[768]{0:T(1024)S(1)}, f32[768]{0:T(1024)}, u32[]{:S(2)}) copy-start(f32[768]{0:T(1024)} %convert_element_type.134) | copy-start | bytes 9220
  288.5 2.3 copy-start.24
  326.6 2.6 copy-start.34
  326.6 2.6 copy-start.22
  332.1 2.8 copy-start.10
  332.1 2.8 copy-start.18
  332.1 211.5 %reduce-scatter.13.cloned.1.call-start = ((), (), s32[]{:S(2)}) async-start(), calls=%async_computation.11 | async-start | bytes 7962624
  335.0 2.6 copy-start.6
  362.5 3.3 copy-start.7
  365.8 2.6 copy-start.6
  393.3 3.4 copy-start.7
  414.8 293.7 %reduce-scatter.9.cloned.1.call-start = ((), (), s32[]{:S(2)}) async-start(), calls=%async_computation.9 | async-start | bytes 10616832 | tf_op jit(solution)/shard_map/reduce_scatter | solution.py:170
  427.3 446.0 %reduce-scatter.11.cloned.1.call-start = ((), (), s32[]{:S(2)}) async-start(), calls=%async_computation.10 | async-start | bytes 10616832 | tf_op jit(solution)/shard_map/reduce_scatter | solution.py:171
  438.9 485.9 %all-reduce.4.cloned.1.call-start = ((), (), s32[]{:S(2)}) async-start(), calls=%async_computation.12 | async-start | bytes 3833856 | tf_op jit(solution)/shard_map/psum | solution.py:206
  444.2 431.3 %copy-start.5 = (f32[1024,768]{1,0:T(8,128)S(1)}, f32[1024,768]{1,0:T(8,128)}, u32[]{:S(2)}) copy-start(f32[1024,768]{1,0:T(8,128)} %copy-done.4) | copy-start | bytes 9437188
  444.2 431.3 %copy-start.23 = (f32[1024]{0:T(1024)S(1)}, f32[1024]{0:T(1024)}, u32[]{:S(2)}) copy-start(f32[1024]{0:T(1024)} %copy-done.22) | copy-start | bytes 12292
  (14 other events, 18.2 us)
Sparse Core Ops, SparseCore 0:
  10.2 67.3 all-gather.4
  79.7 39.8 all-gather.6
  121.8 78.0 all-gather.8
  201.9 77.6 all-gather.10
  332.2 67.9 reduce-scatter.6
  414.9 128.6 reduce-scatter.12
  547.2 161.2 reduce-scatter.8
  712.1 161.1 reduce-scatter.10
  877.1 47.7 all-reduce.3
where the time goes:
time: 944 us; the launch traced here: 940 us
  waiting for transfers between devices  603 us (64%)
  matrix products  173 us (18%)
  other arithmetic  55.7 us (6%)
  local copies, waits for them, and re-layouts  48.9 us (5%)
  blocking collectives  43.5 us (5%)
  between operations  14.5 us (2%)
    reduce_scatter x1, waiting for transfers between devices, body(): lax.psum_scatter(shrink_term, 'fsdp', scatter_dimension=0, tiled=True)  163 us
    reduce_scatter x1, waiting for transfers between devices, body(): lax.psum_scatter(expand_term, 'fsdp', scatter_dimension=0, tiled=True)  163 us
    all_gather x1, waiting for transfers between devices, body(): lax.all_gather(expand_weight, 'fsdp', axis=0, tiled=True)  75.9 us
    all_gather x1, waiting for transfers between devices, body(): lax.all_gather(joint_weight, 'fsdp', axis=0, tiled=True)  57.8 us
    unnamed x10, waiting for transfers between devices  56.7 us
    all_gather x1, waiting for transfers between devices, body(): lax.all_gather(shrink_weight, 'fsdp', axis=0, tiled=True)  43.8 us
    psum x1, blocking collectives, body(): lax.psum((vector_terms[0], vector_terms[1], vector_terms[2], vector_terms...  43.5 us
    psum x1, waiting for transfers between devices, body(): lax.psum(joint_part.astype(jnp.bfloat16), 'rep').astype(jnp.float32)  40.4 us
  transfers between devices with their start and end apart: 9, of which 8 were waited for; matrix products, arithmetic and copies ran while one was open for 22% of the time, Pallas kernels for 0%

commit v1 on v0

--- a/solution.py
+++ b/solution.py
@@ -3,6 +3,7 @@
 import jax.numpy as jnp
 from jax import lax
 from jax.sharding import PartitionSpec as P
+from jax.lax import all_to_all, axis_size
 
 HEADS = 12
 EPS = 1e-12
@@ -122,8 +123,17 @@
         lambda packet: attend_row(packet[0], packet[1]), (joint_low, segment_ids)
     )
     context_low = context.reshape(tok_count, model_width).astype(jnp.bfloat16)
+    build_the_numbers = lambda sheet: jnp.concatenate(
+        all_to_all(
+            jnp.stack([sheet for _ in range(axis_size("fsdp"))], axis=0),
+            axis_name="fsdp",
+            split_axis=0,
+            concat_axis=0,
+        ),
+        axis=0,
+    )
     expand_full, shrink_full = (
-        lax.all_gather(expand_weight, "fsdp", axis=0, tiled=True),
+        build_the_numbers(expand_weight),
         lax.all_gather(shrink_weight, "fsdp", axis=0, tiled=True),
     )
     branch = jnp.dot(

time: 944 us -> 1010 us (1.070)
  waiting for transfers between devices: 603 us -> 644 us
    all_gather x1, waiting for transfers between devices: 57.8 us -> 133 us  [body(): lax.all_gather(joint_weight, 'fsdp', axis=0, tiled=True)]
    all_gather x1, waiting for transfers between devices: 75.9 us -> 44.7 us  [body(): lax.all_gather(expand_weight, 'fsdp', axis=0, tiled=True)]
    dot_general x1, matrix products: 10.1 us -> 21.2 us  [body(): jnp.einsum('tf,df->td', grad_inner, expand_back, preferred_element_type=j...]
    unnamed x69 -> x93, local copies, waits for them, and re-layouts: 19.1 us -> 21.9 us
  transfers between devices with their start and end apart: 9 -> 10, of which waited for: 8 -> 8; matrix products, arithmetic and copies ran while one was open for 22% -> 24% of each run, Pallas kernels for 0% -> 0%
where the time goes in v1:
time: 1010 us; the launch traced here: 996 us
  waiting for transfers between devices  644 us (64%)
  matrix products  181 us (18%)
  local copies, waits for them, and re-layouts  55.5 us (5%)
  other arithmetic  49.1 us (5%)
  blocking collectives  43.5 us (4%)
  between operations  14.8 us (1%)
    reduce_scatter x1, waiting for transfers between devices, body(): lax.psum_scatter(shrink_term, 'fsdp', scatter_dimension=0, tiled=True)  163 us
    reduce_scatter x1, waiting for transfers between devices, body(): lax.psum_scatter(expand_term, 'fsdp', scatter_dimension=0, tiled=True)  163 us
    all_gather x1, waiting for transfers between devices, body(): lax.all_gather(joint_weight, 'fsdp', axis=0, tiled=True)  133 us
    unnamed x10, waiting for transfers between devices  56.7 us
    all_gather x1, waiting for transfers between devices, body(): lax.all_gather(expand_weight, 'fsdp', axis=0, tiled=True)  44.7 us
    psum x1, blocking collectives, body(): lax.psum((vector_terms[0], vector_terms[1], vector_terms[2], vector_terms...  43.5 us
    psum x1, waiting for transfers between devices, body(): lax.psum(joint_part.astype(jnp.bfloat16), 'rep').astype(jnp.float32)  40.4 us
    all_gather x1, waiting for transfers between devices, body(): lax.all_gather(shrink_weight, 'fsdp', axis=0, tiled=True)  39.5 us
  transfers between devices with their start and end apart: 10, of which 8 were waited for; matrix products, arithmetic and copies ran while one was open for 24% of the time, Pallas kernels for 0%

profile of v1, /device:TPU:0, one launch (start us, length us, event | category | flops | bytes accessed | tf_op | source)
XLA Modules:
  0.0 996.4 jit_solution(12374983142267435396)
XLA Ops:
  10.0 3.8 stack.2
  13.8 7.5 all-to-all-start
  25.6 133.2 %all-gather.5.cloned.1.call-done = bf16[768,2304]{1,0:T(8,128)(2,1)} async-done(((bf16[96,2304]{1,0:T(8,128)(2,1)}), bf16[768,2304]{1,0:T(8,128)(2,1)}) %all-gather.5.cloned.1.call-update) | async-done | bytes 3538960 | tf_op jit(solution)/shard_map/all_gather | solution.py:114
  158.8 7.5 add_convert_fusion.1
  166.3 6.7 copy.54
  173.0 23.4 %while.22 = (s32[]{:T(128)}, bf16[2,512,768]{2,1,0:T(8,128)(2,1)}, f32[2,12,512,1]{2,1,3,0:T(8,128)S(1)}, bf16[2,512,2304]{1,2,0:T(8,128)(2,1)}, s32[2,512]{1,0:T(2,128)S(1)}, /*index=5*/s32[]{:T(128)}) while((s32[]{:T(128)}, bf16[2,512,768]{2,1,0:T(8,128)(2,1)}, f32[2,12,512,1]{2,1,3,0:T(8,128)S(1)}, bf16[2,512,2304]{1,2,0:T(8,128)(2,1)}, ...), condition=%wide.region_3.4_spmd, body=%wide.region_0.3_spmd.sunk | while | flops 843311104 | bytes 54753372 | solution.py:122
  179.9 3.6 fusion.98
  191.5 3.6 fusion.98
  196.4 3.9 all-gather.7.cloned.1.call-done
  200.3 3.8 fusion.33
  204.7 36.4 %multiply_convert_fusion.1 = (bf16[1024,3072]{1,0:T(8,128)(2,1)}, f32[1024,3072]{1,0:T(8,128)}, f32[1024,3072]{1,0:T(8,128)}) fusion(f32[3072]{0:T(1024)S(1)} %copy-done.30, bf16[768,3072]{1,0:T(8,128)(2,1)} %bitcast.25, f32[1024,768]{1,0:T(8,128)S(1)} %get-tuple-element.220, f32[768]{0:T(1024)S(1)} %copy-done.21, f32[768]{0:T(1024)S(1)} %copy-done.17, ...), kind=kOutput, calls=%fused_computation.34 | convolution fusion | flops 5043388416 | bytes 39348224 | tf_op jit(solution)/shard_map/dot_general | solution.py:147
  241.1 39.5 %all-gather.9.cloned.1.call-done = bf16[3072,768]{1,0:T(8,128)(2,1)} async-done(((bf16[384,768]{1,0:T(8,128)(2,1)}), bf16[3072,768]{1,0:T(8,128)(2,1)}) %all-gather.9.cloned.1.call-update) | async-done | bytes 4718608 | tf_op jit(solution)/shard_map/all_gather | solution.py:137
  280.6 8.9 fusion.34
  298.2 17.4 %convert_reduce_fusion = (f32[3072]{0:T(1024)}, bf16[1024,3072]{1,0:T(8,128)(2,1)}) fusion(f32[1024,3072]{1,0:T(8,128)} %get-tuple-element.207, bf16[1024,768]{1,0:T(8,128)(2,1)S(1)} %get-tuple-element.199, bf16[3072,768]{1,0:T(8,128)(2,1)} %all-gather.9.cloned.1.call-done, f32[1024,3072]{1,0:T(8,128)} %get-tuple-element.221, f32[3072]{0:T(1024)S(1)} %copy-done.30), kind=kOutput, calls=%fused_computation.32 | convolution fusion | flops 4885312512 | bytes 37773312 | tf_op jit(solution)/shard_map/td,fd->tf/dot_general | solution.py:171
  315.6 44.7 %all-gather.11.cloned.1.call-done = bf16[768,3072]{1,0:T(8,128)(2,1)} async-done(((bf16[96,3072]{1,0:T(8,128)(2,1)}), bf16[768,3072]{1,0:T(8,128)(2,1)}) %all-gather.11.cloned.1.call-update) | async-done | bytes 4718608 | tf_op jit(solution)/shard_map/all_gather | solution.py:163
  360.3 21.2 %multiply_reduce_fusion.1 = (f32[768]{0:T(1024)}, f32[1024]{0:T(1024)S(1)}, f32[768]{0:T(1024)}, f32[1024,768]{1,0:T(8,128)S(1)}) fusion(f32[1024,768]{1,0:T(8,128)S(1)} %get-tuple-element.220, f32[1024]{0:T(1024)S(1)} %fusion.22, f32[1024]{0:T(1024)S(1)} %broadcast_multiply_fusion.1, f32[768]{0:T(1024)S(1)} %copy-done.17, ...), kind=kOutput, calls=%fused_computation.62 | convolution fusion | flops 4839699456 | bytes 20472832 | tf_op jit(solution)/shard_map/tf,df->td/dot_general | solution.py:176
  391.3 61.9 %while.23 = (s32[]{:T(128)}, bf16[2,512,2304]{2,1,0:T(8,128)(2,1)}, bf16[2,512,2304]{1,2,0:T(8,128)(2,1)}, s32[2,512]{1,0:T(2,128)S(1)}, f32[2,12,512,1]{2,1,3,0...) while((s32[]{:T(128)}, bf16[2,512,2304]{2,1,0:T(8,128)(2,1)}, ...), condition=%wide.region_14.15_spmd, body=%wide.region_12.14_spmd.sunk | while | flops 2069358592 | bytes 142784688 | solution.py:195
  399.0 6.8 multiply_reduce_fusion.6
  405.8 7.1 multiply_convert_fusion.3
  418.8 3.4 constant_dynamic-update-slice_fusion.5
  429.8 6.8 multiply_reduce_fusion.6
  436.6 7.2 multiply_convert_fusion.3
  453.2 9.7 convolution_bitcast_fusion
  463.0 8.1 copy.66
  472.9 10.6 %fusion.24 = f32[768,3072]{1,0:T(8,128)} fusion(bf16[1024,3072]{1,0:T(8,128)(2,1)} %get-tuple-element.226, f32[1024,768]{1,0:T(8,128)S(1)} %copy-done.1, f32[768]{0:T(1024)S(1)} %copy-done.22, f32[768]{0:T(1024)S(1)} %copy-done.18, f32[1024]{0:T(1024)S(1)} %copy-done.16, f32[1024]{0:T(1024)S(1)} %copy-done.14), kind=kOutput, calls=%fused_computation.89 | convolution fusion | flops 4835770368 | bytes 18888704 | tf_op jit(solution)/shard_map/td,tf->df/dot_general | solution.py:173
  485.0 10.2 %fusion.37 = f32[3072,768]{1,0:T(8,128)} fusion(bf16[1024,3072]{1,0:T(8,128)(2,1)} %get-tuple-element.206, bf16[1024,768]{1,0:T(8,128)(2,1)S(1)} %copy-done.10), kind=kOutput, calls=%fused_computation.99 | convolution fusion | flops 4831838208 | bytes 17301504 | tf_op jit(solution)/shard_map/tf,td->fd/dot_general | solution.py:170
  500.8 43.5 %all-reduce = (f32[768]{0:T(1024)}, f32[768]{0:T(1024)}, f32[768]{0:T(1024)}, f32[768]{0:T(1024)}, f32[768]{0:T(1024)}, /*index=5*/f32[3072]{0:T(1024)}, f32[768]{0:T(1024)}, f32[768]{0:T(1024)}, f32[768]{0:T(1024)}) all-reduce(f32[768]{0:T(1024)S(1)} %get-tuple-element.157, ...), channel_id=1, replica_groups=mesh['fsdp'=8,'rep'=4] {'fsdp','rep'}, use_global_device_ids=true, to_apply=%region_18.19 | all-reduce | flops 9216 | bytes 73728 | tf_op jit(solution)/shard_map/psum | solution.py:243
  546.0 54.0 %reduce-scatter.13.cloned.1.call-done = f32[96,2304]{1,0:T(8,128)} async-done(((f32[768,2304]{1,0:T(8,128)}), f32[96,2304]{1,0:T(8,128)}) %reduce-scatter.13.cloned.1.call-update) | async-done | bytes 884752
  602.2 162.6 %reduce-scatter.9.cloned.1.call-done = f32[96,3072]{1,0:T(8,128)} async-done(((f32[768,3072]{1,0:T(8,128)}), f32[96,3072]{1,0:T(8,128)}) %reduce-scatter.9.cloned.1.call-update) | async-done | bytes 1179664 | tf_op jit(solution)/shard_map/reduce_scatter | solution.py:180
  767.0 162.7 %reduce-scatter.11.cloned.1.call-done = f32[384,768]{1,0:T(8,128)} async-done(((f32[3072,768]{1,0:T(8,128)}), f32[384,768]{1,0:T(8,128)}) %reduce-scatter.11.cloned.1.call-update) | async-done | bytes 1179664 | tf_op jit(solution)/shard_map/reduce_scatter | solution.py:181
  931.8 9.0 add_add_fusion.4
  940.8 40.4 %all-reduce.4.cloned.1.call-done = (bf16[96,2304]{0,1:T(8,128)(2,1)}, bf16[96,768]{1,0:T(8,128)(2,1)}, bf16[96,3072]{1,0:T(8,128)(2,1)}, bf16[384,768]{1,0:T(8,128)(2,1)}) async-done(((bf16[96,2304]{0,1:T(8,128)(2,1)}, bf16[96,768]{1,0:T(8,128)(2,1)}, bf16[96,3072]{1,0:T(8,128)(2,1)}, bf16[384,768]{1,0:T(8,128)(2,1)}), (bf16[96,2304]{0,1:T(8,128)(2,1)}, bf16[96,768]{1,0:T(8,128)(2,1)}, ...) | async-done | bytes 1769488 | tf_op jit(solution)/shard_map/psum | solution.py:216
  (203 shorter events, 97.4 us)
Async XLA Ops:
  7.2 151.6 %all-gather.5.cloned.1.call-start = ((), (), s32[]{:S(2)}) async-start(), calls=%async_computation.5 | async-start | bytes 3981312 | tf_op jit(solution)/shard_map/all_gather | solution.py:114
  7.9 192.4 %all-gather.7.cloned.1.call-start = ((), (), s32[]{:S(2)}) async-start(), calls=%async_computation.6 | async-start | bytes 1327104 | tf_op jit(solution)/shard_map/all_gather | solution.py:115
  8.7 271.9 %all-gather.9.cloned.1.call-start = ((), (), s32[]{:S(2)}) async-start(), calls=%async_computation.7 | async-start | bytes 5308416 | tf_op jit(solution)/shard_map/all_gather | solution.py:137
  9.4 350.9 %all-gather.11.cloned.1.call-start = ((), (), s32[]{:S(2)}) async-start(), calls=%async_computation.8 | async-start | bytes 5308416 | tf_op jit(solution)/shard_map/all_gather | solution.py:163
  13.7 7.6 copy-start.37
  13.7 8.2 copy-start.38
  13.7 8.8 copy-start.39
  13.7 9.4 copy-start.40
  13.7 10.0 %copy-start.41 = (bf16[768]{0:T(1024)(128)(2,1)S(1)}, bf16[768]{0:T(1024)(128)(2,1)}, u32[]{:S(2)}) copy-start(bf16[768]{0:T(1024)(128)(2,1)} %param.32) | copy-start | bytes 4612
  13.7 10.6 %copy-start.42 = (bf16[768]{0:T(1024)(128)(2,1)S(1)}, bf16[768]{0:T(1024)(128)(2,1)}, u32[]{:S(2)}) copy-start(bf16[768]{0:T(1024)(128)(2,1)} %param.34) | copy-start | bytes 4612
  13.8 11.2 %copy-start.32 = (bf16[3072]{0:T(1024)(128)(2,1)S(1)}, bf16[3072]{0:T(1024)(128)(2,1)}, u32[]{:S(2)}) copy-start(bf16[3072]{0:T(1024)(128)(2,1)} %param.30) | copy-start | bytes 18436
  13.8 11.8 %copy-start.43 = (bf16[768]{0:T(1024)(128)(2,1)S(1)}, bf16[768]{0:T(1024)(128)(2,1)}, u32[]{:S(2)}) copy-start(bf16[768]{0:T(1024)(128)(2,1)} %param.24) | copy-start | bytes 4612
  13.8 11.8 %copy-start.44 = (bf16[768]{0:T(1024)(128)(2,1)S(1)}, bf16[768]{0:T(1024)(128)(2,1)}, u32[]{:S(2)}) copy-start(bf16[768]{0:T(1024)(128)(2,1)} %param.23) | copy-start | bytes 4612
  13.8 145.0 %copy-start.45 = (bf16[2,512,768]{2,1,0:T(8,128)(2,1)S(1)}, bf16[2,512,768]{2,1,0:T(8,128)(2,1)}, u32[]{:S(2)}) copy-start(bf16[2,512,768]{2,1,0:T(8,128)(2,1)} %param.20) | copy-start | bytes 4718596
  13.8 190.8 %all-to-all-start = ((bf16[8,96,3072]{2,1,0:T(8,128)(2,1)}), bf16[8,96,3072]{2,1,0:T(8,128)(2,1)}, u32[]{:S(2)}, u32[]{:S(2)}) async-start(bf16[8,96,3072]{2,1,0:T(8,128)(2,1)} %stack.2), calls=%async_computation | async-start | bytes 9437184 | tf_op jit(solution)/shard_map/all_to_all | solution.py:127
  21.3 523.0 %reduce-scatter.7.cloned.1.call-start = ((), (), s32[]{:S(2)}) async-start(), calls=%async_computation.9 | async-start | bytes 2654208 | tf_op jit(solution)/shard_map/reduce_scatter | solution.py:213
  166.3 6.7 copy-start.19
  173.0 27.3 %copy-start.34 = (f32[768]{0:T(1024)S(1)}, f32[768]{0:T(1024)}, u32[]{:S(2)}) copy-start(f32[768]{0:T(1024)} %convert_element_type.127) | copy-start | bytes 9220
  200.3 4.4 copy-start.21
  200.3 4.4 copy-start.30
  204.1 177.5 %copy-start = (f32[1024,768]{1,0:T(8,128)}, f32[1024,768]{1,0:T(8,128)S(1)}, u32[]{:S(2)}) copy-start(f32[1024,768]{1,0:T(8,128)S(1)} %get-tuple-element.220) | copy-start | bytes 9437188
  204.1 177.4 %copy-start.13 = (f32[1024]{0:T(1024)}, f32[1024]{0:T(1024)S(1)}, u32[]{:S(2)}) copy-start(f32[1024]{0:T(1024)S(1)} %broadcast_multiply_fusion.1) | copy-start | bytes 12292
  204.6 176.9 %copy-start.15 = (f32[1024]{0:T(1024)}, f32[1024]{0:T(1024)S(1)}, u32[]{:S(2)}) copy-start(f32[1024]{0:T(1024)S(1)} %fusion.22) | copy-start | bytes 12292
  204.7 75.9 %copy-start.33 = (f32[768]{0:T(1024)S(1)}, f32[768]{0:T(1024)}, u32[]{:S(2)}) copy-start(f32[768]{0:T(1024)} %convert_element_type.133) | copy-start | bytes 9220
  280.6 9.5 copy-start.2
  280.6 9.5 copy-start.23
  388.6 211.4 %reduce-scatter.13.cloned.1.call-start = ((), (), s32[]{:S(2)}) async-start(), calls=%async_computation.12 | async-start | bytes 7962624
  471.1 293.7 %reduce-scatter.9.cloned.1.call-start = ((), (), s32[]{:S(2)}) async-start(), calls=%async_computation.10 | async-start | bytes 10616832 | tf_op jit(solution)/shard_map/reduce_scatter | solution.py:180
  483.6 446.0 %reduce-scatter.11.cloned.1.call-start = ((), (), s32[]{:S(2)}) async-start(), calls=%async_computation.11 | async-start | bytes 10616832 | tf_op jit(solution)/shard_map/reduce_scatter | solution.py:181
  495.3 485.9 %all-reduce.4.cloned.1.call-start = ((), (), s32[]{:S(2)}) async-start(), calls=%async_computation.13 | async-start | bytes 3833856 | tf_op jit(solution)/shard_map/psum | solution.py:216
  500.5 431.3 %copy-start.5 = (f32[1024,768]{1,0:T(8,128)S(1)}, f32[1024,768]{1,0:T(8,128)}, u32[]{:S(2)}) copy-start(f32[1024,768]{1,0:T(8,128)} %copy-done.4) | copy-start | bytes 9437188
  500.5 431.3 %copy-start.25 = (f32[1024]{0:T(1024)S(1)}, f32[1024]{0:T(1024)}, u32[]{:S(2)}) copy-start(f32[1024]{0:T(1024)} %copy-done.24) | copy-start | bytes 12292
  (27 other events, 54.3 us)
Sparse Core Ops, SparseCore 0:
  10.2 148.5 all-gather.4
  161.0 39.2 all-gather.6
  202.5 78.0 all-gather.8
  282.6 77.6 all-gather.10
  388.7 68.0 reduce-scatter.6
  471.2 128.6 reduce-scatter.12
  603.5 161.2 reduce-scatter.8
  768.4 161.1 reduce-scatter.10
  933.4 47.7 all-reduce.3
